TPU v7x, 128 devices: a whole 4x4x4 slice. The times are simulated.
128 devices in a mesh: patch: 32 (over y, z, x_lo), level: 4 (over x_hi, core).
Axes of the slice: x: 4 (x_hi: 2, x_lo: 2; x = x_hi * 2 + x_lo), y: 4, z: 4, core: 2. Of those that a mesh axis runs over, the one named last changes fastest.
Arguments:
- fields: float32 [6, 64, 32768], P(None, None, ('patch', 'level')), may hold values from -6 to 6
- inv_jacobian: float32 [32768], P(('patch', 'level')), may hold values from 0.5 to 2
- diff_matrix: float32 [3, 64, 64], replicated, may hold values from -0.75 to 0.75
- face_interp: float32 [6, 16, 64], replicated, may hold values from -0.75 to 0.75
- lift_matrix: float32 [6, 64, 16], replicated, may hold values from -1.5 to 1.5
- flux_couple: float32 [6, 6, 6], replicated, may hold values from -2.5 to 2.5
- neighbours: int32 [6, 32768], P(None, ('patch', 'level')), may hold values from 0 to 287
- send_index: int32 [2, 2048], P(None, ('patch', 'level')), may hold values from 0 to 255
- bound_coef: float32 [6], replicated, may hold values from 0.5 to 1.5
- current_coef: float32 [6], replicated, may hold values from -1 to 1
- time_interp: float32 [64], replicated, may hold values from -2 to 2
- current_history: bfloat16 [64, 16384], P(None, ('patch', 'level')), may hold values from -6 to 6
- group_weight: bfloat16 [128, 16384], P(None, ('patch', 'level')), may hold values from -0.1875 to 0.1875
- projection: bfloat16 [16384, 512], P(('patch', 'level')), may hold values from -6 to 6
- kernels: bfloat16 [4, 32, 16, 64], P('level', 'patch'), may hold values from -0.75 to 0.75
- pair_dest: int32 [4, 32, 16], P('level', 'patch'), may hold values from 0 to 31, as said below
- pair_count: int32 [4, 32], P('level', 'patch'), may hold values from 8 to 16
Outputs:
- field_rate: float32 [6, 64, 32768], P(None, None, ('patch', 'level'))
- boundary_field: float32 [64, 16384], P(None, ('patch', 'level'))
Inputs may be any that keep to these rules, and one draw needn't show every extreme that they name: `pair_dest`: in each row the 16 entries are distinct patches, none the row's own patch. Only the first pair_count slots of a group are live. `neighbours`: indices below 256 are the device's own elements, then 16 ghosts from the device below and 16 from the device above along patch+level, wrapping. `send_index`: local element indices of the device.
All inputs are finite; a program needn't handle non-finite values.
Results may differ from a plain program's by a relative error of at most 0.0049.
Values may be sent and summed in bfloat16 or wider, within the bound.
No kernel may reach another device: no remote copies, remote signals or barrier semaphores. Data moves between devices by JAX's collectives and lax.ppermute only.
A program may use at most 192 MiB of HBM per device.

v0:
```python
import math
import jax
import jax.numpy as jnp
from jax import lax
from jax.sharding import PartitionSpec as P

NFP = 16
BE = 8
HIGH = lax.Precision.HIGHEST


def padded_2(array, sides, width):
    edges = {}
    for axis, dim in sides:
        size, length = (lax.axis_size(axis), array.shape[dim])
        up = [(i, (i + 1) % size) for i in range(size)]
        last = lax.slice_in_dim(array, length - width, length, axis=dim)
        leading = lax.slice_in_dim(array, 0, width, axis=dim)
        edges[dim] = (
            lax.ppermute(last, axis, up),
            lax.ppermute(leading, axis, [(b, a) for a, b in up]),
        )
    done = []
    for _, dim in sides:
        low, high = edges[dim]
        around = [(width, width) if d in done else (0, 0) for d in range(array.ndim)]
        array = jnp.concatenate([jnp.pad(low, around), array, jnp.pad(high, around)], axis=dim)
        done.append(dim)
    return array


def side_by_side(arrays, axis, dim, along):
    widths = [math.prod(a.shape[along:]) for a in arrays]
    both = jnp.concatenate(
        [a.reshape(*a.shape[:along], w) for a, w in zip(arrays, widths)], axis=along
    )
    filled = lax.all_gather(both, axis, axis=dim, tiled=True)
    pieces = jnp.split(filled, [sum(widths[:k]) for k in range(1, len(widths))], axis=along)
    return tuple(
        (b.reshape(*filled.shape[:along], *a.shape[along:]) for a, b in zip(arrays, pieces))
    )


def toeplitz(rows):
    count = rows.shape[-1]
    lagged = jnp.arange(count)[:, None] - jnp.arange(count)[None, :]
    picked = jnp.take(rows, jnp.clip(lagged, 0, count - 1), axis=-1)
    return jnp.where(lagged >= 0, picked, jnp.zeros_like(picked))


def per_device(
    fields,
    inv_jacobian,
    diff_matrix,
    face_interp,
    lift_matrix,
    flux_couple,
    neighbours,
    send_index,
    bound_coef,
    current_coef,
    time_interp,
    current_history,
    group_weight,
    projection,
    kernels,
    pair_dest,
    pair_count,
):
    elements = fields.shape[2]
    listed = send_index.shape[1]
    directions = projection.shape[1]
    packed = jnp.take(fields, send_index.reshape(-1), axis=2)
    extended = padded_2(packed.astype(jnp.bfloat16), ((("patch", "level"), 2),), listed).astype(
        packed.dtype
    )
    own = jnp.einsum("fqn,cne->fcqe", face_interp, fields, precision=HIGH)
    newest = jnp.einsum("c,cqe->eq", current_coef, own[5, :, :, :BE], precision=HIGH)
    newest = newest.reshape(1, -1).astype(jnp.bfloat16)
    currents = jnp.concatenate([current_history[1:], newest], axis=0)
    grads = jnp.einsum("rmn,cne->rcme", diff_matrix, fields, precision=HIGH) * inv_jacobian
    electric = jnp.stack(
        [grads[1, 5] - grads[2, 4], grads[2, 3] - grads[0, 5], grads[0, 4] - grads[1, 3]]
    )
    magnetic = -jnp.stack(
        [grads[1, 2] - grads[2, 1], grads[2, 0] - grads[0, 2], grads[0, 1] - grads[1, 0]]
    )
    volume = jnp.concatenate([electric, magnetic], axis=0)
    owner = lax.axis_index("patch") * lax.axis_size("level") + lax.axis_index("level")
    shard_currents, shard_weights, shard_projection = side_by_side(
        (currents[None], group_weight[None], projection[None]), ("patch", "level"), 0, 1
    )
    row = lax.dynamic_index_in_dim(shard_weights, owner, 1, keepdims=False)
    weighted = (shard_currents.astype(jnp.float32) * row.astype(jnp.float32)[:, None, :]).astype(
        jnp.bfloat16
    )
    rays = jnp.einsum("ntb,nbk->tk", weighted, shard_projection, preferred_element_type=jnp.float32)
    rays = rays.astype(jnp.bfloat16)
    patches = lax.axis_size("patch")
    pairs = pair_dest.shape[2]
    live = jnp.arange(pairs) < pair_count[0, 0]
    slots = (pair_dest[0, 0][None, :] == jnp.arange(patches)[:, None]) & live[None, :]
    table = jnp.dot(
        slots.astype(jnp.float32), kernels[0, 0].astype(jnp.float32), precision=HIGH
    ).astype(jnp.bfloat16)
    blocks = jnp.einsum("dts,sk->dtk", toeplitz(table), rays, preferred_element_type=jnp.float32)
    received = lax.all_to_all(blocks, "patch", split_axis=0, concat_axis=0, tiled=True)
    incoming = jnp.sum(received, axis=0)
    incoming = incoming.astype(jnp.bfloat16)
    image = jnp.einsum(
        "ntk,bk->ntb",
        lax.all_gather(incoming[None], ("patch", "level"), axis=0, tiled=True),
        projection,
        preferred_element_type=jnp.float32,
    )
    boundary_field = jnp.einsum(
        "ntb,nb->tb", image, group_weight.astype(jnp.float32), precision=HIGH
    )
    boundary_field = boundary_field * (1.0 / jnp.sqrt(jnp.float32(directions)))
    ghosts = jnp.concatenate([extended[:, :, :listed], extended[:, :, 3 * listed :]], axis=2)
    pool = jnp.concatenate([fields, ghosts], axis=2)
    opposite = face_interp[jnp.array([1, 0, 3, 2, 5, 4])]
    across = pool[:, :, neighbours]
    neighbour = jnp.einsum("fqn,cnfe->fcqe", opposite, across, precision=HIGH)
    interp = jnp.dot(time_interp, boundary_field, precision=HIGH).reshape(BE, NFP)
    exterior = bound_coef[:, None, None] * interp.T[None]
    padded = jnp.pad(exterior, ((0, 0), (0, 0), (0, elements - BE)))
    isbound = (jnp.arange(6)[:, None, None, None] == 5) & (
        jnp.arange(elements)[None, None, None, :] < BE
    )
    neighbour = jnp.where(isbound, padded[None], neighbour)
    flux = jnp.einsum("fcd,fdqe->fcqe", flux_couple, neighbour - own, precision=HIGH)
    surface = jnp.einsum("fnq,fcqe->cne", lift_matrix, flux, precision=HIGH)
    return (volume + surface, boundary_field)


def solution(mesh):
    placed = (
        P(None, None, ("patch", "level")),
        P(("patch", "level")),
        P(),
        P(),
        P(),
        P(),
        P(None, ("patch", "level")),
        P(None, ("patch", "level")),
        P(),
        P(),
        P(),
        P(None, ("patch", "level")),
        P(None, ("patch", "level")),
        P(("patch", "level"), None),
        P("level", "patch", None, None),
        P("level", "patch", None),
        P("level", "patch"),
    )
    return jax.shard_map(
        per_device,
        mesh=mesh,
        in_specs=placed,
        out_specs=(P(None, None, ("patch", "level")), P(None, ("patch", "level"))),
        check_vma=False,
    )
```

profile of v0, /device:TPU:1, one launch (start us, length us, event | category | flops | bytes accessed | tf_op | source)
XLA Modules:
  0.0 635.7 jit_solution(1498488128393288354)
XLA Ops:
  7.2 1.6 convolution_bitcast_fusion.1
  10.5 1.1 copy.98
  12.5 1.1 maximum_bitcast_fusion
  15.4 12.1 %gather_fusion = bf16[4096,32]{1,0:T(8,128)(2,1)S(1)} fusion(bf16[32,64]{0,1:T(8,128)(2,1)S(1)} %copy.59, s32[4096]{0:T(1024)S(1)} %broadcast_clamp_fusion), kind=kCustom, calls=%fused_computation | custom fusion | bytes 540672 | tf_op jit(solution)/shard_map/jit(_take)/gather | solution.py:47
  28.5 247.4 %all-gather.7.cloned.1.call-done = bf16[128,1,90112]{2,1,0:T(2,128)(2,1)} async-done(((bf16[1,1,90112]{2,1,0:T(2,128)(2,1)}), bf16[128,1,90112]{2,1,0:T(2,128)(2,1)}) %all-gather.7.cloned.1.call-update) | async-done | bytes 23068688 | tf_op jit(solution)/shard_map/all_gather | solution.py:37
  275.9 39.5 %copy.117 = bf16[128,1,90112]{2,0,1:T(8,128)(2,1)} copy(bf16[128,1,90112]{2,1,0:T(2,128)(2,1)} %all-gather.7.cloned.1.call-done) | data formatting | bytes 46137344
  315.4 2.5 slice_bitcast_fusion
  317.9 2.0 convert_bitcast_fusion
  319.9 8.0 %split.14 = bf16[128,65536]{1,0:T(8,128)(2,1)S(1)} slice(bf16[128,90112]{1,0:T(8,128)(2,1)} %bitcast.199), slice={[0:128], [24576:90112]} | slice | bytes 33554432 | tf_op jit(solution)/shard_map/split | solution.py:38
  327.9 3.2 copy.100
  331.8 8.8 %copy.101 = bf16[16,8,128,512]{3,2,1,0:T(8,128)(2,1)} copy(bf16[16,8,128,512]{3,1,2,0:T(8,128)(2,1)S(1)} %bitcast.201) | data formatting | bytes 33554432
  340.6 1.0 dynamic-slice_convert_fusion
  342.2 9.7 %fusion.16 = f32[32,64,512]{2,1,0:T(8,128)} fusion(bf16[128,64,128]{2,1,0:T(8,128)(2,1)S(1)} %fusion.2, bf16[128,128,512]{2,1,0:T(8,128)(2,1)} %bitcast.200, bf16[64,64,32]{1,0,2:T(8,128)(2,1)S(1)} %copy.60, pred[64,64]{1,0:T(8,128)(4,1)S(1)} %get-tuple-element.11, pred[64,64]{1,0:T(8,128)(4,1)S(1)} %get-tuple-element.12), kind=kOutput, calls=%fused_computation.25 | convolution fusion | flops 1208254464 | bytes 23339008 | tf_op jit(solution)/shard_map/dts,sk->dtk/dot_general | solution.py:106
  352.0 56.3 %all_to_all.5 = f32[32,64,512]{2,1,0:T(8,128)} all-to-all(f32[32,64,512]{2,1,0:T(8,128)} %fusion.16), channel_id=1, replica_groups=mesh['patch'=32,'level'=4] {'patch'}, dimensions={0} | all-to-all | bytes 8388608 | tf_op jit(solution)/shard_map/all_to_all | solution.py:107
  408.3 3.2 reduce_sum.9
  412.9 4.7 collective-permute-start
  418.3 1.1 fusion.3
  420.8 2.0 collective-permute-done.1
  423.0 5.8 gather_fusion.2
  428.8 183.8 %all-gather.5.cloned.1.call-done = bf16[8192,512]{1,0:T(8,128)(2,1)} async-done(((bf16[64,512]{1,0:T(8,128)(2,1)}), bf16[8192,512]{1,0:T(8,128)(2,1)}) %all-gather.5.cloned.1.call-update) | async-done | bytes 8388624 | tf_op jit(solution)/shard_map/all_gather | solution.py:112
  612.6 5.8 multiply_reduce_fusion
  618.8 7.4 %fusion.10 = f32[6,6,16,256]{3,2,0,1:T(8,128)S(1)} fusion(f32[6,6,16,256]{3,2,0,1:T(8,128)S(1)} %convolution_bitcast_fusion.1, f32[6,64,6,256]{1,0,3,2:T(8,128)} %bitcast.202, f32[6,16,256]{2,1,0:T(8,128)S(1)} %pad.4, pred[6,256]{1,0:T(8,128)(4,1)S(1)} %copy-done.8, f32[6,16,64]{2,1,0:T(8,128)S(1)} %gather_fusion.3), kind=kOutput, calls=%fused_computation.18 | convolution fusion | flops 113541120 | bytes 3663360 | tf_op jit(solution)/shard_map/fqn,cnfe->fcqe/dot_general | solution.py:124
  626.2 1.1 convolution_bitcast_fusion
  627.4 1.5 fusion.13
  (82 shorter events, 9.9 us)
Async XLA Ops:
  7.2 411.1 %copy-start = (f32[3,64,64]{2,1,0:T(8,128)S(1)}, f32[3,64,64]{2,1,0:T(8,128)}, u32[]{:S(2)}) copy-start(f32[3,64,64]{2,1,0:T(8,128)} %param.20) | copy-start | bytes 147460
  7.2 268.7 %all-gather.7.cloned.1.call-start = ((), (), s32[]{:S(2)}) async-start(), calls=%async_computation.2 | async-start | bytes 46497792 | tf_op jit(solution)/shard_map/all_gather | solution.py:37
  13.6 599.0 %all-gather.5.cloned.1.call-start = ((), (), s32[]{:S(2)}) async-start(), calls=%async_computation.1 | async-start | bytes 8454144 | tf_op jit(solution)/shard_map/all_gather | solution.py:112
  408.3 3.3 copy-start.1
  408.3 3.7 copy-start.14
  408.3 9.4 %copy-start.9 = (s32[6,256]{1,0:T(8,128)S(1)}, s32[6,256]{1,0:T(8,128)}, u32[]{:S(2)}) copy-start(s32[6,256]{1,0:T(8,128)} %param.24) | copy-start | bytes 18436
  408.3 10.0 %copy-start.10 = (f32[256]{0:T(256)S(1)}, f32[256]{0:T(256)}, u32[]{:S(2)}) copy-start(f32[256]{0:T(256)} %param.19) | copy-start | bytes 3076
  408.3 11.9 %copy-start.4 = (bf16[128,128]{1,0:T(8,128)(2,1)S(1)}, bf16[128,128]{1,0:T(8,128)(2,1)}, u32[]{:S(2)}) copy-start(bf16[128,128]{1,0:T(8,128)(2,1)} %param.30) | copy-start | bytes 98308
  408.3 11.9 %copy-start.13 = (s32[6]{0:T(128)S(1)}, s32[6]{0:T(128)}, u32[]{:S(2)}) copy-start(s32[6]{0:T(128)} %constant.80) | copy-start | bytes 76
  408.3 11.9 %copy-start.2 = (f32[6,16,64]{2,1,0:T(8,128)S(1)}, f32[6,16,64]{2,1,0:T(8,128)}, u32[]{:S(2)}) copy-start(f32[6,16,64]{2,1,0:T(8,128)} %param.21) | copy-start | bytes 73732
  412.9 7.8 %collective-permute-start = (bf16[6,64,16]{1,0,2:T(8,128)(2,1)S(1)}, bf16[6,64,16]{1,0,2:T(8,128)(2,1)S(1)}, u32[]{:S(2)}, u32[]{:S(2)}) collective-permute-start(bf16[6,64,16]{1,0,2:T(8,128)(2,1)S(1)} %get-tuple-element.9), channel_id=1, source_target_pairs={{0,1},{1,2},{2,3},{3,4},{4,5},{5,6},{6,7},{7,8},{8,9},{9,10},{10,1... | collective-permute-start | bytes 36872 | tf_op jit(solution)/shard_map/ppermute | solution.py:20
  417.7 5.1 collective-permute-start.1
  422.8 189.8 %copy-start.3 = (bf16[128,512]{1,0:T(8,128)(2,1)S(1)}, bf16[128,512]{1,0:T(8,128)(2,1)}, u32[]{:S(2)}) copy-start(bf16[128,512]{1,0:T(8,128)(2,1)} %param.31) | copy-start | bytes 393220
  612.6 5.8 copy-start.11
  612.6 6.1 copy-start.12
  612.6 6.2 copy-start.8
  618.4 7.8 %copy-start.7 = (f32[6,6,6]{2,1,0:T(8,128)S(1)}, f32[6,6,6]{2,1,0:T(8,128)}, u32[]{:S(2)}) copy-start(f32[6,6,6]{2,1,0:T(8,128)} %param.23) | copy-start | bytes 2596
  618.4 9.0 %copy-start.6 = (f32[6,64,16]{1,2,0:T(8,128)S(1)}, f32[6,64,16]{1,2,0:T(8,128)}, u32[]{:S(2)}) copy-start(f32[6,64,16]{1,2,0:T(8,128)} %param.22) | copy-start | bytes 73732
  618.4 10.4 %copy-start.5 = (f32[64,128]{1,0:T(8,128)}, f32[64,128]{1,0:T(8,128)S(1)}, u32[]{:S(2)}) copy-start(f32[64,128]{1,0:T(8,128)S(1)} %multiply_bitcast_fusion) | copy-start | bytes 98308
Sparse Core Ops, SparseCore 0:
  13.7 262.1 all-gather.6
  411.7 200.8 all-gather.4
where the time goes:
time: 636 us
  waiting for transfers between devices  433 us (68%)
  local copies, waits for them, and re-layouts  86.5 us (14%)
  blocking collectives  56.3 us (9%)
  matrix products  29.1 us (5%)
  between operations  15.1 us (2%)
  other arithmetic  10.5 us (2%)
    all_gather x1, waiting for transfers between devices, side_by_side(): filled = lax.all_gather(both, axis, axis=dim, tiled=True)  247 us
    all_gather x1, waiting for transfers between devices, per_device(): lax.all_gather(incoming[None], ('patch', 'level'), axis=0, tiled=True)  184 us
    unnamed x39, local copies, waits for them, and re-layouts  57.1 us
    all_to_all x1, blocking collectives, per_device(): lax.all_to_all(blocks, 'patch', split_axis=0, concat_axis=0, tiled=True)  56.3 us
    gather x2, local copies, waits for them, and re-layouts, toeplitz(): picked = jnp.take(rows, jnp.clip(lagged, 0, count - 1), axis=-1)  13.1 us
  transfers between devices with their start and end apart: 4, of which 3 were waited for; matrix products, arithmetic and copies ran while one was open for 4% of the time, Pallas kernels for 0%

commit v1 on v0

--- a/solution.py
+++ b/solution.py
@@ -7,6 +7,11 @@
 NFP = 16
 BE = 8
 HIGH = lax.Precision.HIGHEST
+
+
+def all_by_exchange(x, mesh_axis, along):
+    outgoing = jnp.stack([x] * lax.axis_size(mesh_axis))
+    return jnp.concatenate(lax.all_to_all(outgoing, mesh_axis, 0, 0), axis=along)
 
 
 def padded_2(array, sides, width):
@@ -109,7 +114,7 @@
     incoming = incoming.astype(jnp.bfloat16)
     image = jnp.einsum(
         "ntk,bk->ntb",
-        lax.all_gather(incoming[None], ("patch", "level"), axis=0, tiled=True),
+        all_by_exchange(incoming[None], ("patch", "level"), 0),
         projection,
         preferred_element_type=jnp.float32,
     )

time: 636 us -> 556 us (0.87); the launches traced: 636 us -> 548 us
  waiting for transfers between devices: 433 us -> 335 us
  starting transfers between devices: 4.81 us -> 11.2 us
    all_gather x1 -> x0, waiting for transfers between devices: 184 us -> none  [per_device(): lax.all_gather(incoming[None], ('patch', 'level'), axis=0, tiled=True)]
    ppermute x1, waiting for transfers between devices: 0.01 us -> 83.1 us  [padded_2(): lax.ppermute(last, axis, up)]
    all_to_all x0 -> x1, starting transfers between devices: none -> 7.9 us  [all_by_exchange(): lax.all_to_all(outgoing, mesh_axis, 0, 0)]
where the time goes in v1:
time: 556 us; the launch traced here: 548 us
  waiting for transfers between devices  335 us (60%)
  local copies, waits for them, and re-layouts  90.8 us (16%)
  blocking collectives  56.3 us (10%)
  matrix products  29.1 us (5%)
  between operations  15.1 us (3%)
  starting transfers between devices  11.2 us (2%)
  other arithmetic  9.89 us (2%)
    all_gather x1, waiting for transfers between devices, side_by_side(): filled = lax.all_gather(both, axis, axis=dim, tiled=True)  248 us
    ppermute x1, waiting for transfers between devices, padded_2(): lax.ppermute(last, axis, up)  83.1 us
    unnamed x39, local copies, waits for them, and re-layouts  57.1 us
    all_to_all x1, blocking collectives, per_device(): lax.all_to_all(blocks, 'patch', split_axis=0, concat_axis=0, tiled=True)  56.3 us
    gather x2, local copies, waits for them, and re-layouts, toeplitz(): picked = jnp.take(rows, jnp.clip(lagged, 0, count - 1), axis=-1)  13.1 us
  transfers between devices with their start and end apart: 4, of which 3 were waited for; matrix products, arithmetic and copies ran while one was open for 4% of the time, Pallas kernels for 0%

profile of v1, /device:TPU:1, one launch (start us, length us, event | category | flops | bytes accessed | tf_op | source)
XLA Modules:
  0.0 547.5 jit_solution(15825027402628239116)
XLA Ops:
  7.2 1.6 convolution_bitcast_fusion.1
  10.5 1.1 copy.117
  12.5 1.1 maximum_bitcast_fusion
  15.3 12.1 %gather_fusion = bf16[4096,32]{1,0:T(8,128)(2,1)S(1)} fusion(bf16[32,64]{0,1:T(8,128)(2,1)S(1)} %copy.78, s32[4096]{0:T(1024)S(1)} %broadcast_clamp_fusion), kind=kCustom, calls=%fused_computation | custom fusion | bytes 540672 | tf_op jit(solution)/shard_map/jit(_take)/gather | solution.py:52
  28.4 247.5 %all-gather.3.cloned.1.call-done = bf16[128,1,90112]{2,1,0:T(2,128)(2,1)} async-done(((bf16[1,1,90112]{2,1,0:T(2,128)(2,1)}), bf16[128,1,90112]{2,1,0:T(2,128)(2,1)}) %all-gather.3.cloned.1.call-update) | async-done | bytes 23068688 | tf_op jit(solution)/shard_map/all_gather | solution.py:42
  276.0 39.5 %copy.136 = bf16[128,1,90112]{2,0,1:T(8,128)(2,1)} copy(bf16[128,1,90112]{2,1,0:T(2,128)(2,1)} %all-gather.3.cloned.1.call-done) | data formatting | bytes 46137344
  315.4 2.5 slice_bitcast_fusion
  317.9 2.0 convert_bitcast_fusion
  320.0 8.0 %split.14 = bf16[128,65536]{1,0:T(8,128)(2,1)S(1)} slice(bf16[128,90112]{1,0:T(8,128)(2,1)} %bitcast.202), slice={[0:128], [24576:90112]} | slice | bytes 33554432 | tf_op jit(solution)/shard_map/split | solution.py:43
  327.9 3.2 copy.119
  331.9 8.7 %copy.120 = bf16[16,8,128,512]{3,2,1,0:T(8,128)(2,1)} copy(bf16[16,8,128,512]{3,1,2,0:T(8,128)(2,1)S(1)} %bitcast.204) | data formatting | bytes 33554432
  342.3 9.7 %fusion.20 = f32[32,64,512]{2,1,0:T(8,128)} fusion(bf16[128,64,128]{2,1,0:T(8,128)(2,1)S(1)} %fusion.4, bf16[128,128,512]{2,1,0:T(8,128)(2,1)} %bitcast.203, bf16[64,64,32]{1,0,2:T(8,128)(2,1)S(1)} %copy.79, pred[64,64]{1,0:T(8,128)(4,1)S(1)} %get-tuple-element.11, pred[64,64]{1,0:T(8,128)(4,1)S(1)} %get-tuple-element.12), kind=kOutput, calls=%fused_computation.27 | convolution fusion | flops 1208254464 | bytes 23339008 | tf_op jit(solution)/shard_map/dts,sk->dtk/dot_general | solution.py:111
  352.0 56.3 %all_to_all.10 = f32[32,64,512]{2,1,0:T(8,128)} all-to-all(f32[32,64,512]{2,1,0:T(8,128)} %fusion.20), channel_id=1, replica_groups=mesh['patch'=32,'level'=4] {'patch'}, dimensions={0} | all-to-all | bytes 8388608 | tf_op jit(solution)/shard_map/all_to_all | solution.py:112
  408.3 2.6 reduce_sum.9
  410.9 4.3 stack.5
  415.2 7.9 %all-to-all-start.1 = ((bf16[128,1,64,512]{3,2,1,0:T(8,128)(2,1)}), bf16[128,1,64,512]{3,2,1,0:T(8,128)(2,1)}, u32[]{:S(2)}, u32[]{:S(2)}) async-start(bf16[128,1,64,512]{3,2,1,0:T(8,128)(2,1)} %stack.5), calls=%async_computation.1 | async-start | bytes 16777216 | tf_op jit(solution)/shard_map/all_to_all | solution.py:14
  424.5 3.2 collective-permute-start
  430.8 83.1 %collective-permute-done = bf16[6,64,16]{1,0,2:T(8,128)(2,1)S(1)} collective-permute-done((bf16[6,64,16]{1,0,2:T(8,128)(2,1)S(1)}, bf16[6,64,16]{1,0,2:T(8,128)(2,1)S(1)}, u32[]{:S(2)}, u32[]{:S(2)}) %collective-permute-start) | collective-permute-done | bytes 12320 | tf_op jit(solution)/shard_map/ppermute | solution.py:25
  513.9 4.5 collective-permute-done.1
  518.6 5.8 %gather_fusion.2 = f32[1536,6,64]{2,1,0:T(8,128)} fusion(f32[6,64,288]{1,0,2:T(8,128)S(1)} %pad_maximum_fusion, s32[2048]{0:T(1024)} %pad_clamp_fusion), kind=kCustom, calls=%fused_computation.2 | custom fusion | bytes 4724736 | tf_op jit(solution)/shard_map/gather | solution.py:128
  524.5 5.8 %multiply_reduce_fusion = f32[128,64]{0,1:T(8,128)S(1)} fusion(bf16[128,1,64,512]{3,2,1,0:T(8,128)(2,1)} %all-to-all-done.1, f32[128,128]{0,1:T(8,128)S(1)} %bitcast_convert_fusion, bf16[128,512]{1,0:T(8,128)(2,1)S(1)} %copy-done.3), kind=kOutput, calls=%fused_computation.12 | convolution fusion | flops 1075830784 | bytes 8617984 | tf_op jit(solution)/shard_map/ntk,bk->ntb/dot_general | solution.py:115
  530.7 7.4 %fusion.14 = f32[6,6,16,256]{3,2,0,1:T(8,128)S(1)} fusion(f32[6,6,16,256]{3,2,0,1:T(8,128)S(1)} %convolution_bitcast_fusion.1, f32[6,64,6,256]{1,0,3,2:T(8,128)} %bitcast.205, f32[6,16,256]{2,1,0:T(8,128)S(1)} %pad.4, pred[6,256]{1,0:T(8,128)(4,1)S(1)} %copy-done.8, f32[6,16,64]{2,1,0:T(8,128)S(1)} %gather_fusion.3), kind=kOutput, calls=%fused_computation.20 | convolution fusion | flops 113541120 | bytes 3663360 | tf_op jit(solution)/shard_map/fqn,cnfe->fcqe/dot_general | solution.py:129
  538.1 1.1 convolution_bitcast_fusion
  539.2 1.5 fusion.17
  (82 shorter events, 11.9 us)
Async XLA Ops:
  7.2 421.2 %copy-start = (f32[3,64,64]{2,1,0:T(8,128)S(1)}, f32[3,64,64]{2,1,0:T(8,128)}, u32[]{:S(2)}) copy-start(f32[3,64,64]{2,1,0:T(8,128)} %param.20) | copy-start | bytes 147460
  7.2 268.8 %all-gather.3.cloned.1.call-start = ((), (), s32[]{:S(2)}) async-start(), calls=%async_computation.2 | async-start | bytes 46497792 | tf_op jit(solution)/shard_map/all_gather | solution.py:42
  415.1 7.9 %copy-start.1 = (f32[6,64,256]{2,1,0:T(8,128)S(1)}, f32[6,64,256]{2,1,0:T(8,128)}, u32[]{:S(2)}) copy-start(f32[6,64,256]{2,1,0:T(8,128)} %param.18) | copy-start | bytes 1179652
  415.1 8.4 %copy-start.14 = (s32[2,16]{1,0:T(2,128)S(1)}, s32[2,16]{1,0:T(2,128)}, u32[]{:S(2)}) copy-start(s32[2,16]{1,0:T(2,128)} %param.25) | copy-start | bytes 388
  415.1 12.5 %copy-start.9 = (s32[6,256]{1,0:T(8,128)S(1)}, s32[6,256]{1,0:T(8,128)}, u32[]{:S(2)}) copy-start(s32[6,256]{1,0:T(8,128)} %param.24) | copy-start | bytes 18436
  415.1 13.2 %copy-start.10 = (f32[256]{0:T(256)S(1)}, f32[256]{0:T(256)}, u32[]{:S(2)}) copy-start(f32[256]{0:T(256)} %param.19) | copy-start | bytes 3076
  415.2 109.3 %all-to-all-start.1 = ((bf16[128,1,64,512]{3,2,1,0:T(8,128)(2,1)}), bf16[128,1,64,512]{3,2,1,0:T(8,128)(2,1)}, u32[]{:S(2)}, u32[]{:S(2)}) async-start(bf16[128,1,64,512]{3,2,1,0:T(8,128)(2,1)} %stack.5), calls=%async_computation.1 | async-start | bytes 16777216 | tf_op jit(solution)/shard_map/all_to_all | solution.py:14
  423.1 7.1 %copy-start.4 = (bf16[128,128]{1,0:T(8,128)(2,1)S(1)}, bf16[128,128]{1,0:T(8,128)(2,1)}, u32[]{:S(2)}) copy-start(bf16[128,128]{1,0:T(8,128)(2,1)} %param.30) | copy-start | bytes 98308
  423.1 7.1 %copy-start.13 = (s32[6]{0:T(128)S(1)}, s32[6]{0:T(128)}, u32[]{:S(2)}) copy-start(s32[6]{0:T(128)} %constant.80) | copy-start | bytes 76
  423.1 7.1 %copy-start.2 = (f32[6,16,64]{2,1,0:T(8,128)S(1)}, f32[6,16,64]{2,1,0:T(8,128)}, u32[]{:S(2)}) copy-start(f32[6,16,64]{2,1,0:T(8,128)} %param.21) | copy-start | bytes 73732
  424.5 89.4 %collective-permute-start = (bf16[6,64,16]{1,0,2:T(8,128)(2,1)S(1)}, bf16[6,64,16]{1,0,2:T(8,128)(2,1)S(1)}, u32[]{:S(2)}, u32[]{:S(2)}) collective-permute-start(bf16[6,64,16]{1,0,2:T(8,128)(2,1)S(1)} %get-tuple-element.9), channel_id=1, source_target_pairs={{0,1},{1,2},{2,3},{3,4},{4,5},{5,6},{6,7},{7,8},{8,9},{9,10},{10,1... | collective-permute-start | bytes 36872 | tf_op jit(solution)/shard_map/ppermute | solution.py:25
  427.7 90.8 %collective-permute-start.1 = (bf16[6,64,16]{1,0,2:T(8,128)(2,1)S(1)}, bf16[6,64,16]{1,0,2:T(8,128)(2,1)S(1)}, u32[]{:S(2)}, u32[]{:S(2)}) collective-permute-start(bf16[6,64,16]{1,0,2:T(8,128)(2,1)S(1)} %get-tuple-element.10), channel_id=1, source_target_pairs={{1,0},{2,1},{3,2},{4,3},{5,4},{6,5},{7,6},{8,7},{9,8},{10,9},{11,1... | collective-permute-start | bytes 36872 | tf_op jit(solution)/shard_map/ppermute | solution.py:26
  518.4 6.0 %copy-start.3 = (bf16[128,512]{1,0:T(8,128)(2,1)S(1)}, bf16[128,512]{1,0:T(8,128)(2,1)}, u32[]{:S(2)}) copy-start(bf16[128,512]{1,0:T(8,128)(2,1)} %param.31) | copy-start | bytes 393220
  524.4 5.8 %copy-start.11 = (f32[64]{0:T(128)S(1)}, f32[64]{0:T(128)}, u32[]{:S(2)}) copy-start(f32[64]{0:T(128)} %param.28) | copy-start | bytes 772
  524.5 6.1 %copy-start.12 = (f32[6]{0:T(128)S(1)}, f32[6]{0:T(128)}, u32[]{:S(2)}) copy-start(f32[6]{0:T(128)} %param.26) | copy-start | bytes 76
  524.5 6.2 %copy-start.8 = (pred[6,256]{1,0:T(8,128)(4,1)S(1)}, pred[6,256]{1,0:T(8,128)(4,1)}, u32[]{:S(2)}) copy-start(pred[6,256]{1,0:T(8,128)(4,1)} %broadcast_and_fusion) | copy-start | bytes 4612
  530.2 7.8 %copy-start.7 = (f32[6,6,6]{2,1,0:T(8,128)S(1)}, f32[6,6,6]{2,1,0:T(8,128)}, u32[]{:S(2)}) copy-start(f32[6,6,6]{2,1,0:T(8,128)} %param.23) | copy-start | bytes 2596
  530.2 9.0 %copy-start.6 = (f32[6,64,16]{1,2,0:T(8,128)S(1)}, f32[6,64,16]{1,2,0:T(8,128)}, u32[]{:S(2)}) copy-start(f32[6,64,16]{1,2,0:T(8,128)} %param.22) | copy-start | bytes 73732
  530.3 10.4 %copy-start.5 = (f32[64,128]{1,0:T(8,128)}, f32[64,128]{1,0:T(8,128)S(1)}, u32[]{:S(2)}) copy-start(f32[64,128]{1,0:T(8,128)S(1)} %multiply_bitcast_fusion) | copy-start | bytes 98308
Sparse Core Ops, SparseCore 0:
  13.7 262.1 all-gather.2
